TPU v7x, 512 devices: a whole 4x4x16 slice. The times are simulated.
512 devices in a mesh: tok: 64 (over z_hi, y, x), head: 8 (over z_lo, core).
Axes of the slice: x: 4, y: 4, z: 16 (z_hi: 4, z_lo: 4; z = z_hi * 4 + z_lo), core: 2. Of those that a mesh axis runs over, the one named last changes fastest.
Arguments:
- hidden_in: bfloat16 [16384, 2560], P('tok'), may hold values from -6 to 6
- norm_gain: float32 [2560], replicated, may hold values from 0.1 to 1.9
- w_qkv: bfloat16 [2560, 3840], P('tok', 'head'), may hold values from -4 to 4
- w_out: bfloat16 [2560, 2560], P('head', 'tok'), may hold values from -0.625 to 0.625
- prefill_cache: bfloat16 [8, 4096, 8, 1280], P(None, 'tok', 'head'), may hold values from -6 to 6
- lengths: int32 [8], replicated, may hold values from 1 to 4096, 20480 in all
- prefill_table: int32 [4096], replicated, may hold values from 0 to 4095, as said below
- decode_table: int32 [4096], replicated, may hold values from 0 to 4095, as said below
Outputs:
- attn_out: bfloat16 [16384, 2560], P('tok', 'head')
- decode_cache: bfloat16 [8, 4096, 8, 1280], P(None, 'tok', 'head')
Inputs may be any that keep to these rules, and one draw needn't show every extreme that they name: `prefill_table`: each prefill slot holds exactly one logical block. `decode_table`: the block in prefill slot s * 64 + k goes to decode slot d * 64 + k, where d - s modulo the size of tok depends only on k and each residue occurs for exactly 1 values of k.
All inputs are finite; a program needn't handle non-finite values.
Results may differ from a plain program's by a relative error of at most 0.015.
The roundings to bfloat16 on the way count: a program that leaves them out, or rounds other values in their place, can miss the bound.
Values may be sent and summed in bfloat16 or wider, within the bound.
A program may use at most 64 MiB of HBM per device.

v0:
```python
import math
import jax
import jax.numpy as jnp
from jax import lax
from jax.sharding import PartitionSpec as P

HD = 80
QPK = 4
BLK = 8
NORM_EPS = 1e-05
ROPE_BASE = 1000000.0


def rotary(vectors, positions):
    half_width = vectors.shape[-1] // 2
    frequency = ROPE_BASE ** (-2.0 * jnp.arange(half_width, dtype=jnp.float32) / vectors.shape[-1])
    angles = positions.astype(jnp.float32)[:, None] * frequency[None, :]
    cosine = jnp.cos(angles)[:, None, :]
    sines = jnp.sin(angles)[:, None, :]
    front_half = vectors[..., :half_width]
    back_half = vectors[..., half_width:]
    return jnp.concatenate(
        [front_half * cosine - back_half * sines, back_half * cosine + front_half * sines], axis=-1
    )


def attend(hidden_in, norm_gain, w_qkv):
    tok_rows = hidden_in.shape[0]
    my_index = lax.axis_index("tok")
    float_rows = hidden_in.astype(jnp.float32)
    normed = (
        float_rows
        * lax.rsqrt(jnp.mean(float_rows * float_rows, axis=-1, keepdims=True) + NORM_EPS)
        * norm_gain
    ).astype(jnp.bfloat16)
    projected = jnp.dot(
        normed, lax.all_gather(w_qkv, "tok", axis=0, tiled=True), preferred_element_type=jnp.float32
    )
    kv_local = w_qkv.shape[1] // ((QPK + 2) * HD)
    projected = projected.reshape(tok_rows, kv_local, QPK + 2, HD)
    row_index = jnp.arange(tok_rows, dtype=jnp.int32)
    positions = my_index * tok_rows + row_index
    queries = (
        rotary(projected[:, :, :QPK].reshape(tok_rows, kv_local * QPK, HD), positions)
        .astype(jnp.bfloat16)
        .reshape(tok_rows, kv_local * QPK * HD)
    )
    key_rows = (
        rotary(projected[:, :, QPK], positions)
        .astype(jnp.bfloat16)
        .reshape(tok_rows, kv_local * HD)
    )
    values = projected[:, :, QPK + 1].astype(jnp.bfloat16).reshape(tok_rows, kv_local * HD)
    query_grid = (
        queries.reshape(tok_rows, kv_local, QPK, HD)
        .transpose(1, 2, 0, 3)
        .reshape(kv_local, QPK * tok_rows, HD)
    )
    query_pos = jnp.tile(positions, QPK)
    last_row = jnp.max(positions)
    scale_factor = 1.0 / math.sqrt(HD)

    def key_positions(block_start, count):
        whole_rows = block_start + jnp.arange(count, dtype=jnp.int32)
        return whole_rows

    initial = (
        jnp.full((kv_local, QPK * tok_rows), -1e30, jnp.float32),
        jnp.zeros((kv_local, QPK * tok_rows), jnp.float32),
        jnp.zeros((kv_local, QPK * tok_rows, HD), jnp.float32),
    )
    key_part = lax.all_gather(key_rows, "tok", axis=0, tiled=True)
    value_part = lax.all_gather(values, "tok", axis=0, tiled=True)
    row_count = key_part.shape[0]
    step_rows = math.gcd(row_count, 512)
    key_grid = key_part.reshape(row_count, kv_local, HD)
    value_grid = value_part.reshape(row_count, kv_local, HD)

    def advance(step_index, status):
        offset = step_index * step_rows
        key_pos = key_positions(offset, step_rows)

        def update(current):
            running, denominator, weighted = current
            key_block = lax.dynamic_slice_in_dim(key_grid, offset, step_rows, 0)
            value_block = lax.dynamic_slice_in_dim(value_grid, offset, step_rows, 0)
            scores = (
                jnp.einsum(
                    "hqd,khd->hqk", query_grid, key_block, preferred_element_type=jnp.float32
                )
                * scale_factor
            )
            allowed = (key_pos[None, :] <= query_pos[:, None])[None]
            masked = jnp.where(allowed, scores, -1e30)
            highest = jnp.maximum(running, jnp.max(masked, axis=-1))
            expo_terms = jnp.where(allowed, jnp.exp(masked - highest[..., None]), 0.0)
            shrink = jnp.exp(running - highest)
            denominator = denominator * shrink + jnp.sum(expo_terms, axis=-1)
            weighted = weighted * shrink[..., None] + jnp.einsum(
                "hqk,khd->hqd",
                expo_terms.astype(jnp.bfloat16),
                value_block,
                preferred_element_type=jnp.float32,
            )
            return (highest, denominator, weighted)

        return lax.cond(jnp.min(key_pos) > last_row, lambda unchanged: unchanged, update, status)

    running, denominator, weighted = lax.fori_loop(0, row_count // step_rows, advance, initial)
    context = (
        (weighted / denominator[..., None])
        .reshape(kv_local, QPK, tok_rows, HD)
        .transpose(2, 0, 1, 3)
    )
    context = context.reshape(tok_rows, kv_local * QPK * HD).astype(jnp.bfloat16)
    return context


def project_out(context, w_out):
    partial_value = jnp.dot(
        context,
        lax.all_gather(w_out, "tok", axis=1, tiled=True),
        preferred_element_type=jnp.float32,
    )
    return lax.psum_scatter(
        partial_value.astype(jnp.bfloat16), "head", scatter_dimension=1, tiled=True
    )


def hand_over(prefill_cache, lengths, prefill_table, decode_table):
    tok_count = lax.axis_size("tok")
    my_index = lax.axis_index("tok")
    layers, slot_count, kv_local, extent = prefill_cache.shape
    block_total = prefill_table.shape[0]
    request_count = lengths.shape[0]
    per_request = block_total // request_count
    every_block = jnp.arange(block_total, dtype=jnp.int32)
    logical_of = jnp.zeros((block_total,), jnp.int32).at[prefill_table].set(every_block)
    held_here = lax.dynamic_slice_in_dim(logical_of, my_index * slot_count, slot_count)
    request = held_here // per_request
    request_len = jnp.sum(
        jnp.where(
            request[:, None] == jnp.arange(request_count, dtype=jnp.int32)[None, :],
            lengths[None, :],
            0,
        ),
        axis=1,
    )
    live_rows = (held_here % per_request * BLK)[:, None] + jnp.arange(BLK, dtype=jnp.int32)[
        None, :
    ] < request_len[:, None]
    masked = prefill_cache.reshape(layers, slot_count, kv_local, BLK, extent // BLK) * live_rows[
        None, :, None, :, None
    ].astype(jnp.bfloat16)
    masked = masked.reshape(layers, slot_count, kv_local, extent)
    target = decode_table[held_here] // slot_count
    send_order = jnp.argsort(target * slot_count + jnp.arange(slot_count, dtype=jnp.int32))
    outgoing = jnp.take(masked, send_order, axis=1)
    per_peer = slot_count // tok_count
    decode_of = jnp.zeros((block_total,), jnp.int32).at[decode_table].set(every_block)
    arriving = lax.dynamic_slice_in_dim(decode_of, my_index * slot_count, slot_count)
    anchor = prefill_table[arriving]
    position = jnp.argsort(jnp.argsort(anchor))
    collected = []
    for layer_index in range(layers):
        sending = outgoing[layer_index].reshape(tok_count, per_peer, kv_local, extent)
        received = lax.all_to_all(sending, "tok", split_axis=0, concat_axis=0, tiled=True)
        collected.append(received.reshape(slot_count, kv_local, extent))
    incoming = jnp.stack(collected)
    return jnp.take(incoming, position, axis=1)


def on_device(
    hidden_in, norm_gain, w_qkv, w_out, prefill_cache, lengths, prefill_table, decode_table
):
    context = attend(hidden_in, norm_gain, w_qkv)
    attn_out = project_out(context, w_out)
    decode_cache = hand_over(prefill_cache, lengths, prefill_table, decode_table)
    return (attn_out, decode_cache)


def solution(mesh):
    in_specs = (
        P("tok", None),
        P(),
        P("tok", "head"),
        P("head", "tok"),
        P(None, "tok", "head", None),
        P(),
        P(),
        P(),
    )
    out_specs = (P("tok", "head"), P(None, "tok", "head", None))
    return jax.shard_map(
        on_device, mesh=mesh, in_specs=in_specs, out_specs=out_specs, check_vma=False
    )
```

profile of v0, /device:TPU:64, one launch (start us, length us, event | category | flops | bytes accessed | tf_op | source)
XLA Modules:
  0.0 723.2 jit_solution(4846801455397867306)
XLA Ops:
  8.0 1.7 fusion.24
  9.7 124.3 %all-gather.6.cloned.1.call-done = bf16[2560,480]{1,0:T(8,128)(2,1)} async-done(((bf16[40,480]{1,0:T(8,128)(2,1)}), bf16[2560,480]{1,0:T(8,128)(2,1)}) %all-gather.6.cloned.1.call-update) | async-done | bytes 2457616 | tf_op jit(solution)/shard_map/all_gather | solution.py:37
  134.0 3.4 fusion.27
  139.1 15.5 %scatter_custom_fusion = s32[4096]{0:T(1024)S(1)} fusion(s32[4096]{0:T(1024)S(1)} %compare_select_fusion.3, s32[4096]{0:T(1024)S(1)} %iota.52, s32[]{:T(128)} %copy.199), kind=kCustom, calls=%fused_computation.84 | custom fusion | bytes 16388 | tf_op jit(solution)/shard_map/scatter | solution.py:138
  154.6 15.5 %scatter_custom_fusion.1 = s32[4096]{0:T(1024)S(1)} fusion(s32[4096]{0:T(1024)S(1)} %compare_select_fusion.2, s32[4096]{0:T(1024)S(1)} %iota.55, s32[]{:T(128)} %copy.199), kind=kCustom, calls=%fused_computation.82 | custom fusion | bytes 16388 | tf_op jit(solution)/shard_map/scatter | solution.py:160
  171.0 0.8 gather_fusion
  171.7 2.0 sort.45
  173.8 0.8 fusion.29
  175.5 2.4 slice_bitcast_fusion
  178.5 1.6 reduce.4
  180.1 0.7 reshape.360
  180.8 10.3 %all-to-all-start = ((bf16[64,2,640]{2,1,0:T(2,128)(2,1)}), bf16[64,2,640]{2,1,0:T(2,128)(2,1)S(1)}, u32[]{:S(2)}, u32[]{:S(2)}) async-start(bf16[64,2,640]{2,1,0:T(2,128)(2,1)} %reshape.360), calls=%async_computation.1 | async-start | bytes 327680 | tf_op jit(solution)/shard_map/all_to_all | solution.py:167
  191.1 1.6 reduce.5
  193.5 17.4 %all-to-all-done = bf16[64,2,640]{2,1,0:T(2,128)(2,1)S(1)} async-done(((bf16[64,2,640]{2,1,0:T(2,128)(2,1)}), bf16[64,2,640]{2,1,0:T(2,128)(2,1)S(1)}, u32[]{:S(2)}, u32[]{:S(2)}) %all-to-all-start) | async-done | bytes 163872 | tf_op jit(solution)/shard_map/all_to_all | solution.py:167
  210.8 6.8 all-to-all-start.1
  218.2 1.6 reduce.6
  220.8 22.2 %all-to-all-done.1 = bf16[64,2,640]{2,1,0:T(2,128)(2,1)S(1)} async-done(((bf16[64,2,640]{2,1,0:T(2,128)(2,1)}), bf16[64,2,640]{2,1,0:T(2,128)(2,1)S(1)}, u32[]{:S(2)}, u32[]{:S(2)}) %all-to-all-start.1) | async-done | bytes 163872 | tf_op jit(solution)/shard_map/all_to_all | solution.py:167
  242.9 4.6 all-to-all-start.2
  248.2 1.6 reduce.7
  250.5 1.6 reduce.8
  252.2 0.7 reshape.368
  253.2 13.7 %all-to-all-done.2 = bf16[64,2,640]{2,1,0:T(2,128)(2,1)S(1)} async-done(((bf16[64,2,640]{2,1,0:T(2,128)(2,1)}), bf16[64,2,640]{2,1,0:T(2,128)(2,1)S(1)}, u32[]{:S(2)}, u32[]{:S(2)}) %all-to-all-start.2) | async-done | bytes 163872 | tf_op jit(solution)/shard_map/all_to_all | solution.py:167
  266.9 14.7 %all-to-all-start.3 = ((bf16[64,2,640]{2,1,0:T(2,128)(2,1)}), bf16[64,2,640]{2,1,0:T(2,128)(2,1)S(1)}, u32[]{:S(2)}, u32[]{:S(2)}) async-start(bf16[64,2,640]{2,1,0:T(2,128)(2,1)} %reshape.366), calls=%async_computation.4 | async-start | bytes 327680 | tf_op jit(solution)/shard_map/all_to_all | solution.py:167
  281.6 3.3 all-gather.8.cloned.1.call-done
  284.9 130.3 %all-gather.12.cloned.1.call-done = bf16[16384,1,1,80]{0,3,2,1:T(8,128)(2,1)} async-done(((bf16[256,1,1,80]{0,3,2,1:T(8,128)(2,1)}), bf16[16384,1,1,80]{0,3,2,1:T(8,128)(2,1)}) %all-gather.12.cloned.1.call-update) | async-done | bytes 2621456 | tf_op jit(solution)/shard_map/all_gather | solution.py:73
  415.3 64.7 %while.18 = (s32[]{:T(128)}, f32[1,1024]{1,0:T(1,128)S(1)}, f32[1,1024]{1,0:T(1,128)S(1)}, f32[1,1024,80]{1,2,0:T(8,128)S(1)}, s32[]{:T(128)}, /*index=5*/bf16[1...) while((s32[]{:T(128)}, f32[1,1024]{1,0:T(1,128)S(1)}, ...), condition=%wide.region_8.9_spmd.clone, body=%wide.region_2.8_spmd.clone.sunk | while | flops 176327680 | bytes 7374129 | solution.py:109
  417.1 3.8 conditional.3
  417.2 1.4 fusion.2
  419.2 1.6 fusion.5
  480.0 137.3 %all-to-all-start.4 = ((bf16[64,2,640]{2,1,0:T(2,128)(2,1)}), bf16[64,2,640]{2,1,0:T(2,128)(2,1)S(1)}, u32[]{:S(2)}, u32[]{:S(2)}) async-start(bf16[64,2,640]{2,1,0:T(2,128)(2,1)} %reshape.368), calls=%async_computation.5 | async-start | bytes 327680 | tf_op jit(solution)/shard_map/all_to_all | solution.py:167
  617.6 3.4 convolution_convert_fusion
  621.1 1.6 reduce.9
  623.4 12.6 %all-to-all-done.4 = bf16[64,2,640]{2,1,0:T(2,128)(2,1)S(1)} async-done(((bf16[64,2,640]{2,1,0:T(2,128)(2,1)}), bf16[64,2,640]{2,1,0:T(2,128)(2,1)S(1)}, u32[]{:S(2)}, u32[]{:S(2)}) %all-to-all-start.4) | async-done | bytes 163872 | tf_op jit(solution)/shard_map/all_to_all | solution.py:167
  636.0 5.1 all-to-all-start.5
  641.2 1.6 reduce.10
  643.5 18.4 %all-to-all-done.5 = bf16[64,2,640]{2,1,0:T(2,128)(2,1)S(1)} async-done(((bf16[64,2,640]{2,1,0:T(2,128)(2,1)}), bf16[64,2,640]{2,1,0:T(2,128)(2,1)S(1)}, u32[]{:S(2)}, u32[]{:S(2)}) %all-to-all-start.5) | async-done | bytes 163872 | tf_op jit(solution)/shard_map/all_to_all | solution.py:167
  661.9 4.6 all-to-all-start.6
  666.5 1.6 reduce.11
  668.9 15.6 %all-to-all-done.6 = bf16[64,2,640]{2,1,0:T(2,128)(2,1)S(1)} async-done(((bf16[64,2,640]{2,1,0:T(2,128)(2,1)}), bf16[64,2,640]{2,1,0:T(2,128)(2,1)S(1)}, u32[]{:S(2)}, u32[]{:S(2)}) %all-to-all-start.6) | async-done | bytes 163872 | tf_op jit(solution)/shard_map/all_to_all | solution.py:167
  684.5 4.6 all-to-all-start.7
  689.1 0.8 gather_fusion.1
  689.9 2.0 sort.46
  691.9 2.0 sort.47
  694.8 0.8 reshape.373
  695.6 11.5 %all-to-all-done.7 = bf16[64,2,640]{2,1,0:T(2,128)(2,1)S(1)} async-done(((bf16[64,2,640]{2,1,0:T(2,128)(2,1)}), bf16[64,2,640]{2,1,0:T(2,128)(2,1)S(1)}, u32[]{:S(2)}, u32[]{:S(2)}) %all-to-all-start.7) | async-done | bytes 163872 | tf_op jit(solution)/shard_map/all_to_all | solution.py:167
  707.1 0.9 reshape.375
  708.0 6.6 stack.3
  715.4 1.3 copy.174
  (211 shorter events, 35.5 us)
Async XLA Ops:
  7.2 126.8 %all-gather.6.cloned.1.call-start = ((), (), s32[]{:S(2)}) async-start(), calls=%async_computation.9 | async-start | bytes 2662400 | tf_op jit(solution)/shard_map/all_gather | solution.py:37
  7.9 277.0 %all-gather.8.cloned.1.call-start = ((), (), s32[]{:S(2)}) async-start(), calls=%async_computation.10 | async-start | bytes 2662400 | tf_op jit(solution)/shard_map/all_gather | solution.py:72
  9.6 129.4 %copy-start.1 = (s32[4096]{0:T(1024)S(1)}, s32[4096]{0:T(1024)}, u32[]{:S(2)}) copy-start(s32[4096]{0:T(1024)} %param.20) | copy-start | bytes 49156
  9.7 145.0 %copy-start = (s32[4096]{0:T(1024)S(1)}, s32[4096]{0:T(1024)}, u32[]{:S(2)}) copy-start(s32[4096]{0:T(1024)} %param.21) | copy-start | bytes 49156
  9.7 160.7 %copy-start.3 = (s32[8]{0:T(128)S(1)}, s32[8]{0:T(128)}, u32[]{:S(2)}) copy-start(s32[8]{0:T(128)} %param.19) | copy-start | bytes 100
  137.4 36.4 %copy-start.2 = (bf16[8,64,1,1280]{3,1,2,0:T(8,128)(2,1)S(1)}, bf16[8,64,1,1280]{3,1,2,0:T(8,128)(2,1)}, u32[]{:S(2)}) copy-start(bf16[8,64,1,1280]{3,1,2,0:T(8,128)(2,1)} %param.18) | copy-start | bytes 3932164
  138.3 276.9 %all-gather.12.cloned.1.call-start = ((), (), s32[]{:S(2)}) async-start(), calls=%async_computation.13 | async-start | bytes 2662400 | tf_op jit(solution)/shard_map/all_gather | solution.py:73
  180.8 30.0 %all-to-all-start = ((bf16[64,2,640]{2,1,0:T(2,128)(2,1)}), bf16[64,2,640]{2,1,0:T(2,128)(2,1)S(1)}, u32[]{:S(2)}, u32[]{:S(2)}) async-start(bf16[64,2,640]{2,1,0:T(2,128)(2,1)} %reshape.360), calls=%async_computation.1 | async-start | bytes 327680 | tf_op jit(solution)/shard_map/all_to_all | solution.py:167
  210.8 32.1 %all-to-all-start.1 = ((bf16[64,2,640]{2,1,0:T(2,128)(2,1)}), bf16[64,2,640]{2,1,0:T(2,128)(2,1)S(1)}, u32[]{:S(2)}, u32[]{:S(2)}) async-start(bf16[64,2,640]{2,1,0:T(2,128)(2,1)} %reshape.362), calls=%async_computation.2 | async-start | bytes 327680 | tf_op jit(solution)/shard_map/all_to_all | solution.py:167
  217.6 400.0 %all-gather.10.cloned.1.call-start = ((), (), s32[]{:S(2)}) async-start(), calls=%async_computation.11 | async-start | bytes 1996800 | tf_op jit(solution)/shard_map/all_gather | solution.py:122
  242.9 23.9 %all-to-all-start.2 = ((bf16[64,2,640]{2,1,0:T(2,128)(2,1)}), bf16[64,2,640]{2,1,0:T(2,128)(2,1)S(1)}, u32[]{:S(2)}, u32[]{:S(2)}) async-start(bf16[64,2,640]{2,1,0:T(2,128)(2,1)} %reshape.364), calls=%async_computation.3 | async-start | bytes 327680 | tf_op jit(solution)/shard_map/all_to_all | solution.py:167
  266.9 213.1 %all-to-all-start.3 = ((bf16[64,2,640]{2,1,0:T(2,128)(2,1)}), bf16[64,2,640]{2,1,0:T(2,128)(2,1)S(1)}, u32[]{:S(2)}, u32[]{:S(2)}) async-start(bf16[64,2,640]{2,1,0:T(2,128)(2,1)} %reshape.366), calls=%async_computation.4 | async-start | bytes 327680 | tf_op jit(solution)/shard_map/all_to_all | solution.py:167
  480.0 156.0 %all-to-all-start.4 = ((bf16[64,2,640]{2,1,0:T(2,128)(2,1)}), bf16[64,2,640]{2,1,0:T(2,128)(2,1)S(1)}, u32[]{:S(2)}, u32[]{:S(2)}) async-start(bf16[64,2,640]{2,1,0:T(2,128)(2,1)} %reshape.368), calls=%async_computation.5 | async-start | bytes 327680 | tf_op jit(solution)/shard_map/all_to_all | solution.py:167
  617.3 99.3 %reduce-scatter.2.cloned.1.call-start = ((), (), s32[]{:S(2)}) async-start(), calls=%async_computation.12 | async-start | bytes 1474560 | tf_op jit(solution)/shard_map/reduce_scatter | solution.py:125
  636.0 25.9 %all-to-all-start.5 = ((bf16[64,2,640]{2,1,0:T(2,128)(2,1)}), bf16[64,2,640]{2,1,0:T(2,128)(2,1)S(1)}, u32[]{:S(2)}, u32[]{:S(2)}) async-start(bf16[64,2,640]{2,1,0:T(2,128)(2,1)} %reshape.370), calls=%async_computation.6 | async-start | bytes 327680 | tf_op jit(solution)/shard_map/all_to_all | solution.py:167
  661.9 22.6 %all-to-all-start.6 = ((bf16[64,2,640]{2,1,0:T(2,128)(2,1)}), bf16[64,2,640]{2,1,0:T(2,128)(2,1)S(1)}, u32[]{:S(2)}, u32[]{:S(2)}) async-start(bf16[64,2,640]{2,1,0:T(2,128)(2,1)} %reshape.372), calls=%async_computation.7 | async-start | bytes 327680 | tf_op jit(solution)/shard_map/all_to_all | solution.py:167
  684.5 22.6 %all-to-all-start.7 = ((bf16[64,2,640]{2,1,0:T(2,128)(2,1)}), bf16[64,2,640]{2,1,0:T(2,128)(2,1)S(1)}, u32[]{:S(2)}, u32[]{:S(2)}) async-start(bf16[64,2,640]{2,1,0:T(2,128)(2,1)} %reshape.374), calls=%async_computation.8 | async-start | bytes 327680 | tf_op jit(solution)/shard_map/all_to_all | solution.py:167
Sparse Core Ops, SparseCore 0:
  12.2 121.7 all-gather.5
  138.4 146.4 all-gather.7
  288.9 126.2 all-gather.11
  419.3 116.7 all-gather.9
  621.2 42.9 reduce-scatter.1
where the time goes:
time: 727 us; the launch traced here: 723 us
  waiting for transfers between devices  370 us (51%)
  starting transfers between devices  188 us (26%)
  local copies, waits for them, and re-layouts  54.5 us (7%)
  other arithmetic  46 us (6%)
  loops' own time  39.5 us (5%)
  between operations  14.3 us (2%)
  matrix products  9.89 us (1%)
    all_to_all x8, starting transfers between devices, hand_over(): lax.all_to_all(sending, 'tok', split_axis=0, concat_axis=0, tiled=True)  188 us
    all_gather x1, waiting for transfers between devices, attend(): value_part = lax.all_gather(values, 'tok', axis=0, tiled=True)  130 us
    all_gather x1, waiting for transfers between devices, attend(): lax.all_gather(w_qkv, 'tok', axis=0, tiled=True)  124 us
    all_to_all x8, waiting for transfers between devices, hand_over(): lax.all_to_all(sending, 'tok', split_axis=0, concat_axis=0, tiled=True)  111 us
    another operation x1, loops' own time, attend(): lax.fori_loop(0, row_count // step_rows, advance, initial)  38.6 us
    add x32, other arithmetic, key_positions(): whole_rows = block_start + jnp.arange(count, dtype=jnp.int32)  21.3 us
    scatter x1, local copies, waits for them, and re-layouts, hand_over(): jnp.zeros((block_total,), jnp.int32).at[decode_table].set(every_block)  15.5 us
    scatter x1, local copies, waits for them, and re-layouts, hand_over(): jnp.zeros((block_total,), jnp.int32).at[prefill_table].set(every_block)  15.5 us
  transfers between devices with their start and end apart: 13, of which 10 were waited for; matrix products, arithmetic and copies ran while one was open for 15% of the time, Pallas kernels for 0%

commit v1 on v0

--- a/solution.py
+++ b/solution.py
@@ -1,3 +1,4 @@
+import functools
 import math
 import jax
 import jax.numpy as jnp
@@ -9,6 +10,17 @@
 BLK = 8
 NORM_EPS = 1e-05
 ROPE_BASE = 1000000.0
+
+
+def meet_the_stocks(here_x, dev_axis):
+    in_order = []
+    for _ in range(lax.axis_size(dev_axis)):
+        in_order.append(here_x)
+    n_now = jnp.concatenate(lax.all_to_all(jnp.stack(in_order), dev_axis, 0, 0), axis=0)
+    return n_now
+
+
+divide_lanes = functools.partial(meet_the_stocks, dev_axis="tok")
 
 
 def rotary(vectors, positions):
@@ -33,9 +45,7 @@
         * lax.rsqrt(jnp.mean(float_rows * float_rows, axis=-1, keepdims=True) + NORM_EPS)
         * norm_gain
     ).astype(jnp.bfloat16)
-    projected = jnp.dot(
-        normed, lax.all_gather(w_qkv, "tok", axis=0, tiled=True), preferred_element_type=jnp.float32
-    )
+    projected = jnp.dot(normed, divide_lanes(w_qkv), preferred_element_type=jnp.float32)
     kv_local = w_qkv.shape[1] // ((QPK + 2) * HD)
     projected = projected.reshape(tok_rows, kv_local, QPK + 2, HD)
     row_index = jnp.arange(tok_rows, dtype=jnp.int32)

time: 727 us -> 741 us (1.019)
  starting transfers between devices: 188 us -> 199 us
    all_gather x1 -> x0, waiting for transfers between devices: 124 us -> none  [attend(): lax.all_gather(w_qkv, 'tok', axis=0, tiled=True)]
    all_to_all x0 -> x1, waiting for transfers between devices: none -> 120 us  [meet_the_stocks(): lax.all_to_all(jnp.stack(in_order), dev_axis, 0, 0)]
    all_to_all x0 -> x1, starting transfers between devices: none -> 19.4 us  [meet_the_stocks(): lax.all_to_all(jnp.stack(in_order), dev_axis, 0, 0)]
    all_to_all x8, waiting for transfers between devices: 111 us -> 123 us  [hand_over(): lax.all_to_all(sending, 'tok', split_axis=0, concat_axis=0, tiled=True)]
    all_to_all x8, starting transfers between devices: 188 us -> 179 us  [hand_over(): lax.all_to_all(sending, 'tok', split_axis=0, concat_axis=0, tiled=True)]
    all_gather x1, waiting for transfers between devices: 130 us -> 122 us  [attend(): value_part = lax.all_gather(values, 'tok', axis=0, tiled=True)]
  transfers between devices with their start and end apart: 13 -> 13, of which waited for: 10 -> 9; matrix products, arithmetic and copies ran while one was open for 15% -> 15% of each run, Pallas kernels for 0% -> 0%
where the time goes in v1:
time: 741 us; the launch traced here: 737 us
  waiting for transfers between devices  367 us (50%)
  starting transfers between devices  199 us (27%)
  local copies, waits for them, and re-layouts  59.6 us (8%)
  other arithmetic  47.7 us (6%)
  loops' own time  39.5 us (5%)
  between operations  14.2 us (2%)
  matrix products  9.55 us (1%)
    all_to_all x8, starting transfers between devices, hand_over(): lax.all_to_all(sending, 'tok', split_axis=0, concat_axis=0, tiled=True)  179 us
    all_to_all x8, waiting for transfers between devices, hand_over(): lax.all_to_all(sending, 'tok', split_axis=0, concat_axis=0, tiled=True)  123 us
    all_gather x1, waiting for transfers between devices, attend(): value_part = lax.all_gather(values, 'tok', axis=0, tiled=True)  122 us
    all_to_all x1, waiting for transfers between devices, meet_the_stocks(): lax.all_to_all(jnp.stack(in_order), dev_axis, 0, 0)  120 us
    another operation x1, loops' own time, attend(): lax.fori_loop(0, row_count // step_rows, advance, initial)  38.6 us
    add x32, other arithmetic, key_positions(): whole_rows = block_start + jnp.arange(count, dtype=jnp.int32)  21.3 us
    all_to_all x1, starting transfers between devices, meet_the_stocks(): lax.all_to_all(jnp.stack(in_order), dev_axis, 0, 0)  19.4 us
    scatter x1, local copies, waits for them, and re-layouts, hand_over(): jnp.zeros((block_total,), jnp.int32).at[prefill_table].set(every_block)  15.5 us
  transfers between devices with their start and end apart: 13, of which 9 were waited for; matrix products, arithmetic and copies ran while one was open for 15% of the time, Pallas kernels for 0%

profile of v1, /device:TPU:64, one launch (start us, length us, event | category | flops | bytes accessed | tf_op | source)
XLA Modules:
  0.0 736.7 jit_solution(1561148487673639273)
XLA Ops:
  7.2 2.5 stack.4
  9.6 19.4 %all-to-all-start = ((bf16[64,40,480]{2,1,0:T(8,128)(2,1)}), bf16[64,40,480]{2,1,0:T(8,128)(2,1)S(1)}, u32[]{:S(2)}, u32[]{:S(2)}) async-start(bf16[64,40,480]{2,1,0:T(8,128)(2,1)} %stack.4), calls=%async_computation | async-start | bytes 5242880 | tf_op jit(solution)/shard_map/all_to_all | solution.py:19
  29.1 1.7 fusion.24
  30.8 120.5 %all-to-all-done = bf16[64,40,480]{2,1,0:T(8,128)(2,1)S(1)} async-done(((bf16[64,40,480]{2,1,0:T(8,128)(2,1)}), bf16[64,40,480]{2,1,0:T(8,128)(2,1)S(1)}, u32[]{:S(2)}, u32[]{:S(2)}) %all-to-all-start) | async-done | bytes 2457632 | tf_op jit(solution)/shard_map/all_to_all | solution.py:19
  151.3 2.7 copy.167
  154.0 3.0 fusion.33
  158.7 15.5 %scatter_custom_fusion = s32[4096]{0:T(1024)S(1)} fusion(s32[4096]{0:T(1024)S(1)} %compare_select_fusion.3, s32[4096]{0:T(1024)S(1)} %iota.52, s32[]{:T(128)} %copy.214), kind=kCustom, calls=%fused_computation.86 | custom fusion | bytes 16388 | tf_op jit(solution)/shard_map/scatter | solution.py:148
  174.3 15.5 %scatter_custom_fusion.1 = s32[4096]{0:T(1024)S(1)} fusion(s32[4096]{0:T(1024)S(1)} %compare_select_fusion.2, s32[4096]{0:T(1024)S(1)} %iota.55, s32[]{:T(128)} %copy.214), kind=kCustom, calls=%fused_computation.84 | custom fusion | bytes 16388 | tf_op jit(solution)/shard_map/scatter | solution.py:170
  190.6 0.8 gather_fusion
  191.4 2.0 sort.45
  193.4 2.1 fusion.30
  196.4 2.4 slice_bitcast_fusion
  199.4 1.7 reduce.4
  201.8 7.7 %all-to-all-start.1 = ((bf16[64,2,640]{2,1,0:T(2,128)(2,1)}), bf16[64,2,640]{2,1,0:T(2,128)(2,1)S(1)}, u32[]{:S(2)}, u32[]{:S(2)}) async-start(bf16[64,2,640]{2,1,0:T(2,128)(2,1)} %reshape.371), calls=%async_computation.2 | async-start | bytes 327680 | tf_op jit(solution)/shard_map/all_to_all | solution.py:177
  209.5 1.7 reduce.5
  211.9 18.2 %all-to-all-done.1 = bf16[64,2,640]{2,1,0:T(2,128)(2,1)S(1)} async-done(((bf16[64,2,640]{2,1,0:T(2,128)(2,1)}), bf16[64,2,640]{2,1,0:T(2,128)(2,1)S(1)}, u32[]{:S(2)}, u32[]{:S(2)}) %all-to-all-start.1) | async-done | bytes 163872 | tf_op jit(solution)/shard_map/all_to_all | solution.py:177
  230.0 6.5 all-to-all-start.2
  237.3 1.7 reduce.6
  239.9 27.7 %all-to-all-done.2 = bf16[64,2,640]{2,1,0:T(2,128)(2,1)S(1)} async-done(((bf16[64,2,640]{2,1,0:T(2,128)(2,1)}), bf16[64,2,640]{2,1,0:T(2,128)(2,1)S(1)}, u32[]{:S(2)}, u32[]{:S(2)}) %all-to-all-start.2) | async-done | bytes 163872 | tf_op jit(solution)/shard_map/all_to_all | solution.py:177
  267.6 6.3 all-to-all-start.3
  274.5 1.7 reduce.7
  276.9 1.7 reduce.8
  279.5 19.8 %all-to-all-done.3 = bf16[64,2,640]{2,1,0:T(2,128)(2,1)S(1)} async-done(((bf16[64,2,640]{2,1,0:T(2,128)(2,1)}), bf16[64,2,640]{2,1,0:T(2,128)(2,1)S(1)}, u32[]{:S(2)}, u32[]{:S(2)}) %all-to-all-start.3) | async-done | bytes 163872 | tf_op jit(solution)/shard_map/all_to_all | solution.py:177
  299.4 7.4 all-to-all-start.4
  306.7 122.2 %all-gather.9.cloned.1.call-done = bf16[16384,1,1,80]{0,3,2,1:T(8,128)(2,1)} async-done(((bf16[256,1,1,80]{0,3,2,1:T(8,128)(2,1)}), bf16[16384,1,1,80]{0,3,2,1:T(8,128)(2,1)}) %all-gather.9.cloned.1.call-update) | async-done | bytes 2621456 | tf_op jit(solution)/shard_map/all_gather | solution.py:83
  429.0 64.7 %while.18 = (s32[]{:T(128)}, f32[1,1024]{1,0:T(1,128)S(1)}, f32[1,1024]{1,0:T(1,128)S(1)}, f32[1,1024,80]{1,2,0:T(8,128)S(1)}, s32[]{:T(128)}, /*index=5*/bf16[1...) while((s32[]{:T(128)}, f32[1,1024]{1,0:T(1,128)S(1)}, ...), condition=%wide.region_8.9_spmd.clone, body=%wide.region_2.8_spmd.clone.sunk | while | flops 176327680 | bytes 7374129 | solution.py:119
  430.9 3.8 conditional.3
  430.9 1.4 fusion.2
  433.0 1.6 fusion.5
  493.8 137.3 %all-to-all-start.5 = ((bf16[64,2,640]{2,1,0:T(2,128)(2,1)}), bf16[64,2,640]{2,1,0:T(2,128)(2,1)S(1)}, u32[]{:S(2)}, u32[]{:S(2)}) async-start(bf16[64,2,640]{2,1,0:T(2,128)(2,1)} %reshape.379), calls=%async_computation.6 | async-start | bytes 327680 | tf_op jit(solution)/shard_map/all_to_all | solution.py:177
  631.4 3.4 convolution_convert_fusion
  634.8 1.7 reduce.9
  637.2 12.6 %all-to-all-done.5 = bf16[64,2,640]{2,1,0:T(2,128)(2,1)S(1)} async-done(((bf16[64,2,640]{2,1,0:T(2,128)(2,1)}), bf16[64,2,640]{2,1,0:T(2,128)(2,1)S(1)}, u32[]{:S(2)}, u32[]{:S(2)}) %all-to-all-start.5) | async-done | bytes 163872 | tf_op jit(solution)/shard_map/all_to_all | solution.py:177
  649.8 5.2 all-to-all-start.6
  655.0 1.7 reduce.10
  657.4 18.4 %all-to-all-done.6 = bf16[64,2,640]{2,1,0:T(2,128)(2,1)S(1)} async-done(((bf16[64,2,640]{2,1,0:T(2,128)(2,1)}), bf16[64,2,640]{2,1,0:T(2,128)(2,1)S(1)}, u32[]{:S(2)}, u32[]{:S(2)}) %all-to-all-start.6) | async-done | bytes 163872 | tf_op jit(solution)/shard_map/all_to_all | solution.py:177
  675.8 4.6 all-to-all-start.7
  680.4 1.7 reduce.11
  682.8 15.3 %all-to-all-done.7 = bf16[64,2,640]{2,1,0:T(2,128)(2,1)S(1)} async-done(((bf16[64,2,640]{2,1,0:T(2,128)(2,1)}), bf16[64,2,640]{2,1,0:T(2,128)(2,1)S(1)}, u32[]{:S(2)}, u32[]{:S(2)}) %all-to-all-start.7) | async-done | bytes 163872 | tf_op jit(solution)/shard_map/all_to_all | solution.py:177
  698.0 4.6 all-to-all-start.8
  702.7 0.8 gather_fusion.1
  703.5 2.0 sort.46
  705.5 2.0 sort.47
  708.3 0.8 reshape.384
  709.2 11.5 %all-to-all-done.8 = bf16[64,2,640]{2,1,0:T(2,128)(2,1)S(1)} async-done(((bf16[64,2,640]{2,1,0:T(2,128)(2,1)}), bf16[64,2,640]{2,1,0:T(2,128)(2,1)S(1)}, u32[]{:S(2)}, u32[]{:S(2)}) %all-to-all-start.8) | async-done | bytes 163872 | tf_op jit(solution)/shard_map/all_to_all | solution.py:177
  720.6 0.9 reshape.386
  721.5 6.6 stack.5
  728.9 1.3 copy.189
  (212 shorter events, 36.3 us)
Async XLA Ops:
  9.6 141.6 %all-to-all-start = ((bf16[64,40,480]{2,1,0:T(8,128)(2,1)}), bf16[64,40,480]{2,1,0:T(8,128)(2,1)S(1)}, u32[]{:S(2)}, u32[]{:S(2)}) async-start(bf16[64,40,480]{2,1,0:T(8,128)(2,1)} %stack.4), calls=%async_computation | async-start | bytes 5242880 | tf_op jit(solution)/shard_map/all_to_all | solution.py:19
  29.0 277.7 %all-gather.5.cloned.1.call-start = ((), (), s32[]{:S(2)}) async-start(), calls=%async_computation.10 | async-start | bytes 2662400 | tf_op jit(solution)/shard_map/all_gather | solution.py:82
  151.3 2.7 copy-start.2
  154.0 4.7 copy-start.1
  154.0 20.3 %copy-start = (s32[4096]{0:T(1024)S(1)}, s32[4096]{0:T(1024)}, u32[]{:S(2)}) copy-start(s32[4096]{0:T(1024)} %param.21) | copy-start | bytes 49156
  154.0 36.0 %copy-start.3 = (s32[8]{0:T(128)S(1)}, s32[8]{0:T(128)}, u32[]{:S(2)}) copy-start(s32[8]{0:T(128)} %param.19) | copy-start | bytes 100
  157.9 271.1 %all-gather.9.cloned.1.call-start = ((), (), s32[]{:S(2)}) async-start(), calls=%async_computation.13 | async-start | bytes 2662400 | tf_op jit(solution)/shard_map/all_gather | solution.py:83
  201.8 28.2 %all-to-all-start.1 = ((bf16[64,2,640]{2,1,0:T(2,128)(2,1)}), bf16[64,2,640]{2,1,0:T(2,128)(2,1)S(1)}, u32[]{:S(2)}, u32[]{:S(2)}) async-start(bf16[64,2,640]{2,1,0:T(2,128)(2,1)} %reshape.371), calls=%async_computation.2 | async-start | bytes 327680 | tf_op jit(solution)/shard_map/all_to_all | solution.py:177
  230.0 37.6 %all-to-all-start.2 = ((bf16[64,2,640]{2,1,0:T(2,128)(2,1)}), bf16[64,2,640]{2,1,0:T(2,128)(2,1)S(1)}, u32[]{:S(2)}, u32[]{:S(2)}) async-start(bf16[64,2,640]{2,1,0:T(2,128)(2,1)} %reshape.373), calls=%async_computation.3 | async-start | bytes 327680 | tf_op jit(solution)/shard_map/all_to_all | solution.py:177
  236.5 394.8 %all-gather.7.cloned.1.call-start = ((), (), s32[]{:S(2)}) async-start(), calls=%async_computation.11 | async-start | bytes 1996800 | tf_op jit(solution)/shard_map/all_gather | solution.py:132
  267.6 31.8 %all-to-all-start.3 = ((bf16[64,2,640]{2,1,0:T(2,128)(2,1)}), bf16[64,2,640]{2,1,0:T(2,128)(2,1)S(1)}, u32[]{:S(2)}, u32[]{:S(2)}) async-start(bf16[64,2,640]{2,1,0:T(2,128)(2,1)} %reshape.375), calls=%async_computation.4 | async-start | bytes 327680 | tf_op jit(solution)/shard_map/all_to_all | solution.py:177
  299.4 194.4 %all-to-all-start.4 = ((bf16[64,2,640]{2,1,0:T(2,128)(2,1)}), bf16[64,2,640]{2,1,0:T(2,128)(2,1)S(1)}, u32[]{:S(2)}, u32[]{:S(2)}) async-start(bf16[64,2,640]{2,1,0:T(2,128)(2,1)} %reshape.377), calls=%async_computation.5 | async-start | bytes 327680 | tf_op jit(solution)/shard_map/all_to_all | solution.py:177
  493.8 156.0 %all-to-all-start.5 = ((bf16[64,2,640]{2,1,0:T(2,128)(2,1)}), bf16[64,2,640]{2,1,0:T(2,128)(2,1)S(1)}, u32[]{:S(2)}, u32[]{:S(2)}) async-start(bf16[64,2,640]{2,1,0:T(2,128)(2,1)} %reshape.379), calls=%async_computation.6 | async-start | bytes 327680 | tf_op jit(solution)/shard_map/all_to_all | solution.py:177
  631.1 99.1 %reduce-scatter.2.cloned.1.call-start = ((), (), s32[]{:S(2)}) async-start(), calls=%async_computation.12 | async-start | bytes 1474560 | tf_op jit(solution)/shard_map/reduce_scatter | solution.py:135
  649.8 26.0 %all-to-all-start.6 = ((bf16[64,2,640]{2,1,0:T(2,128)(2,1)}), bf16[64,2,640]{2,1,0:T(2,128)(2,1)S(1)}, u32[]{:S(2)}, u32[]{:S(2)}) async-start(bf16[64,2,640]{2,1,0:T(2,128)(2,1)} %reshape.381), calls=%async_computation.7 | async-start | bytes 327680 | tf_op jit(solution)/shard_map/all_to_all | solution.py:177
  675.8 22.3 %all-to-all-start.7 = ((bf16[64,2,640]{2,1,0:T(2,128)(2,1)}), bf16[64,2,640]{2,1,0:T(2,128)(2,1)S(1)}, u32[]{:S(2)}, u32[]{:S(2)}) async-start(bf16[64,2,640]{2,1,0:T(2,128)(2,1)} %reshape.383), calls=%async_computation.8 | async-start | bytes 327680 | tf_op jit(solution)/shard_map/all_to_all | solution.py:177
  698.0 22.6 %all-to-all-start.8 = ((bf16[64,2,640]{2,1,0:T(2,128)(2,1)}), bf16[64,2,640]{2,1,0:T(2,128)(2,1)S(1)}, u32[]{:S(2)}, u32[]{:S(2)}) async-start(bf16[64,2,640]{2,1,0:T(2,128)(2,1)} %reshape.385), calls=%async_computation.9 | async-start | bytes 327680 | tf_op jit(solution)/shard_map/all_to_all | solution.py:177
Sparse Core Ops, SparseCore 0:
  158.0 145.8 all-gather.4
  307.9 121.0 all-gather.8
  433.2 113.8 all-gather.6
  635.0 42.9 reduce-scatter.1
